TPU v7x, 32 devices: a whole 2x2x4 slice. The times are simulated.
32 devices in a mesh: samples: 8 (over z, y), snps: 4 (over x, core).
Axes of the slice: x: 2, y: 2, z: 4, core: 2. Of those that a mesh axis runs over, the one named last changes fastest.
Arguments:
- genotype: int32 [4096, 1536], P('samples', 'snps'), may hold values from 0 to 2
- mask: int32 [4096, 1536], P('samples', 'snps'), may hold values 0 or 1
Outputs:
- blocks: float32 [4096, 2560], P('samples', 'snps')
All inputs are finite; a program needn't handle non-finite values. No bound on the sum of `mask` on one device may be relied on, other than what follows from the above.
Results may differ from a plain program's by a relative error of at most 0.0014.
Values may be sent and summed in bfloat16 or wider, within the bound.
A program may use at most 128 MiB of HBM per device.

v0:
```python
import math
import jax
import jax.numpy as jnp
from jax import lax
from jax.sharding import PartitionSpec as P


def standardize(dosage, observed_mask, allele_sum, observed_sum):
    frequency = (allele_sum + 1.0) / (2.0 * observed_sum + 2.0)
    scaled = (
        observed_mask * (dosage - 2.0 * frequency) / jnp.sqrt(2.0 * frequency * (1.0 - frequency))
    )
    return scaled.astype(jnp.bfloat16)


def cross_block(own_rows, other_rows):
    return lax.dot_general(
        own_rows, other_rows, (((1,), (1,)), ((), ())), preferred_element_type=jnp.float32
    )


def rows_for_columns(full_rows, offsets):
    circle_size = lax.axis_size("samples")
    parts = lax.axis_size("snps")
    block_rows = full_rows.shape[0]
    width = offsets * block_rows // parts
    piece = math.gcd(block_rows, width)
    per_block = block_rows // piece
    per_part = width // piece
    part = lax.axis_index("snps")
    pieces = []
    for index in range(per_part):
        sub = (part * per_part + index) % per_block
        sent = lax.dynamic_slice_in_dim(full_rows, sub * piece, piece, axis=0)
        pairs = []
        for row in range(circle_size):
            for column in range(parts):
                ahead = (column * per_part + index) // per_block
                source = (row + ahead) % circle_size
                pairs.append((source * parts + column, row * parts + column))
        pieces.append(lax.ppermute(sent, ("samples", "snps"), pairs))
    return jnp.concatenate(pieces, axis=0)


def per_device(genotype, mask):
    dosage = genotype.astype(jnp.float32)
    observed_mask = mask.astype(jnp.float32)
    allele_sum, observed_sum = lax.psum(
        (jnp.sum(dosage * observed_mask, axis=0), jnp.sum(observed_mask, axis=0)), "samples"
    )
    standard = standardize(dosage, observed_mask, allele_sum, observed_sum)
    offsets = lax.axis_size("samples") // 2 + 1
    full_rows = lax.all_gather(standard, "snps", axis=1, tiled=True)
    others = rows_for_columns(full_rows, offsets)
    return cross_block(full_rows, others) / full_rows.shape[1]


def solution(mesh):
    return jax.shard_map(
        per_device,
        mesh=mesh,
        in_specs=(P("samples", "snps"), P("samples", "snps")),
        out_specs=P("samples", "snps"),
        check_vma=False,
    )
```

profile of v0, /device:TPU:3, one launch (start us, length us, event | category | flops | bytes accessed | tf_op | source)
XLA Modules:
  0.0 140.2 jit_solution(2090311282719203152)
XLA Ops:
  6.5 0.0 copy-start.1
  6.5 0.0 copy-start
  6.5 0.0 all-gather.2.cloned.1.call-start
  6.5 1.6 %multiply_reduce_fusion = (f32[384]{0:T(512)S(1)}, f32[384]{0:T(512)S(1)}) fusion(s32[512,384]{1,0:T(8,128)} %param.2, s32[512,384]{1,0:T(8,128)} %param.3), kind=kLoop, calls=%fused_computation.2 | loop fusion | flops 982272 | bytes 1575936 | tf_op jit(solution)/shard_map/reduce_sum | solution.py:49
  8.2 17.9 %all-reduce = (f32[384]{0:T(512)S(1)}, f32[384]{0:T(512)S(1)}) all-reduce(f32[384]{0:T(512)S(1)} %get-tuple-element.6, f32[384]{0:T(512)S(1)} %get-tuple-element.5), channel_id=1, replica_groups=mesh['samples'=8,'snps'=4] {'samples'}, use_global_device_ids=true, to_apply=%region_3.0 | all-reduce | flops 768 | bytes 6144 | tf_op jit(solution)/shard_map/psum | solution.py:48
  26.1 0.0 copy-done.1
  26.1 0.0 copy-done
  26.1 0.9 divide_convert_fusion
  27.0 0.0 all-gather.2.cloned.1.call-update
  27.1 20.0 %all-gather.2.cloned.1.call-done = bf16[512,1536]{1,0:T(8,128)(2,1)} async-done(((bf16[512,384]{1,0:T(8,128)(2,1)}), bf16[512,1536]{1,0:T(8,128)(2,1)}) %all-gather.2.cloned.1.call-update) | async-done | bytes 1572880 | tf_op jit(solution)/shard_map/all_gather | solution.py:53
  47.1 1.6 %constant_dynamic-slice_fusion = (bf16[128,1536]{1,0:T(8,128)(2,1)S(1)}, bf16[128,1536]{1,0:T(8,128)(2,1)S(1)}, bf16[128,1536]{1,0:T(8,128)(2,1)S(1)}, bf16[128,1536]{1,0:T(8,128)(2,1)S(1)}, bf16[128,1536]{1,0:T(8,128)(2,1)S(1)}) fusion(bf16[512,1536]{1,0:T(8,128)(2,1)} %all-gather.2.cloned.1.call-done, s32[]{:T(128)S(6)} %select_n.47, s32[]{:T(128)S(6)} %select_n.45, ...), kind=kLoop, calls=%fused_computation.11 | loop fusion | bytes 3932180 | tf_op jit(solution)/shard_map/dynamic_slice | solution.py:34
  48.7 5.2 %collective-permute-start = (bf16[128,1536]{1,0:T(8,128)(2,1)S(1)}, bf16[128,1536]{1,0:T(8,128)(2,1)S(1)}, u32[]{:S(2)}, u32[]{:S(2)}) collective-permute-start(bf16[128,1536]{1,0:T(8,128)(2,1)S(1)} %get-tuple-element.15), channel_id=1, source_target_pairs={{0,0},{5,1},{10,2},{15,3},{4,4},{9,5},{14,6},{19,7},{8,8},{13,9},{... | collective-permute-start | bytes 1179656 | tf_op jit(solution)/shard_map/ppermute | solution.py:41
  53.9 2.1 %collective-permute-start.1 = (bf16[128,1536]{1,0:T(8,128)(2,1)S(1)}, bf16[128,1536]{1,0:T(8,128)(2,1)S(1)}, u32[]{:S(2)}, u32[]{:S(2)}) collective-permute-start(bf16[128,1536]{1,0:T(8,128)(2,1)S(1)} %get-tuple-element.14), channel_id=1, source_target_pairs={{0,0},{5,1},{10,2},{19,3},{4,4},{9,5},{14,6},{23,7},{8,8},{13,9},{... | collective-permute-start | bytes 1179656 | tf_op jit(solution)/shard_map/ppermute | solution.py:41
  56.0 2.2 %collective-permute-start.4 = (bf16[128,1536]{1,0:T(8,128)(2,1)S(1)}, bf16[128,1536]{1,0:T(8,128)(2,1)S(1)}, u32[]{:S(2)}, u32[]{:S(2)}) collective-permute-start(bf16[128,1536]{1,0:T(8,128)(2,1)S(1)} %get-tuple-element.11), channel_id=1, source_target_pairs={{4,0},{9,1},{14,2},{19,3},{8,4},{13,5},{18,6},{23,7},{12,8},{17,9}... | collective-permute-start | bytes 1179656 | tf_op jit(solution)/shard_map/ppermute | solution.py:41
  58.2 2.1 %collective-permute-start.3 = (bf16[128,1536]{1,0:T(8,128)(2,1)S(1)}, bf16[128,1536]{1,0:T(8,128)(2,1)S(1)}, u32[]{:S(2)}, u32[]{:S(2)}) collective-permute-start(bf16[128,1536]{1,0:T(8,128)(2,1)S(1)} %get-tuple-element.12), channel_id=1, source_target_pairs={{0,0},{9,1},{14,2},{19,3},{4,4},{13,5},{18,6},{23,7},{8,8},{17,9},... | collective-permute-start | bytes 1179656 | tf_op jit(solution)/shard_map/ppermute | solution.py:41
  60.3 0.0 copy-start.2
  60.3 4.2 %collective-permute-start.2 = (bf16[128,1536]{1,0:T(8,128)(2,1)S(1)}, bf16[128,1536]{1,0:T(8,128)(2,1)S(1)}, u32[]{:S(2)}, u32[]{:S(2)}) collective-permute-start(bf16[128,1536]{1,0:T(8,128)(2,1)S(1)} %get-tuple-element.13), channel_id=1, source_target_pairs={{0,0},{5,1},{14,2},{19,3},{4,4},{9,5},{18,6},{23,7},{8,8},{13,9},{... | collective-permute-start | bytes 1179656 | tf_op jit(solution)/shard_map/ppermute | solution.py:41
  64.5 0.0 collective-permute-done
  64.6 41.0 %collective-permute-done.1 = bf16[128,1536]{1,0:T(8,128)(2,1)S(1)} collective-permute-done((bf16[128,1536]{1,0:T(8,128)(2,1)S(1)}, bf16[128,1536]{1,0:T(8,128)(2,1)S(1)}, u32[]{:S(2)}, u32[]{:S(2)}) %collective-permute-start.1) | collective-permute-done | bytes 393248 | tf_op jit(solution)/shard_map/ppermute | solution.py:41
  105.6 25.1 %collective-permute-done.2 = bf16[128,1536]{1,0:T(8,128)(2,1)S(1)} collective-permute-done((bf16[128,1536]{1,0:T(8,128)(2,1)S(1)}, bf16[128,1536]{1,0:T(8,128)(2,1)S(1)}, u32[]{:S(2)}, u32[]{:S(2)}) %collective-permute-start.2) | collective-permute-done | bytes 393248 | tf_op jit(solution)/shard_map/ppermute | solution.py:41
  130.7 0.0 collective-permute-done.3
  130.8 0.0 collective-permute-done.4
  130.8 0.0 copy-done.2
  130.8 2.5 %convolution_multiply_fusion = f32[512,640]{1,0:T(8,128)} fusion(bf16[512,1536]{1,0:T(8,128)(2,1)S(1)} %copy-done.2, bf16[640,1536]{1,0:T(8,128)(2,1)S(1)} %constant_dynamic-update-slice_fusion), kind=kOutput, calls=%fused_computation | convolution fusion | flops 1006960640 | bytes 4849664 | tf_op jit(solution)/shard_map/dot_general | solution.py:17
  (7 shorter events, 0.2 us)
Async XLA Ops:
  6.5 19.6 %copy-start.1 = (s32[512,384]{1,0:T(8,128)S(1)}, s32[512,384]{1,0:T(8,128)}, u32[]{:S(2)}) copy-start(s32[512,384]{1,0:T(8,128)} %param.3) | copy-start | bytes 2359300
  6.5 19.6 %copy-start = (s32[512,384]{1,0:T(8,128)S(1)}, s32[512,384]{1,0:T(8,128)}, u32[]{:S(2)}) copy-start(s32[512,384]{1,0:T(8,128)} %param.2) | copy-start | bytes 2359300
  6.5 40.6 %all-gather.2.cloned.1.call-start = ((), (), s32[]{:S(2)}) async-start(), calls=%async_computation | async-start | bytes 1966080 | tf_op jit(solution)/shard_map/all_gather | solution.py:53
  48.7 15.8 %collective-permute-start = (bf16[128,1536]{1,0:T(8,128)(2,1)S(1)}, bf16[128,1536]{1,0:T(8,128)(2,1)S(1)}, u32[]{:S(2)}, u32[]{:S(2)}) collective-permute-start(bf16[128,1536]{1,0:T(8,128)(2,1)S(1)} %get-tuple-element.15), channel_id=1, source_target_pairs={{0,0},{5,1},{10,2},{15,3},{4,4},{9,5},{14,6},{19,7},{8,8},{13,9},{... | collective-permute-start | bytes 1179656 | tf_op jit(solution)/shard_map/ppermute | solution.py:41
  53.9 51.7 %collective-permute-start.1 = (bf16[128,1536]{1,0:T(8,128)(2,1)S(1)}, bf16[128,1536]{1,0:T(8,128)(2,1)S(1)}, u32[]{:S(2)}, u32[]{:S(2)}) collective-permute-start(bf16[128,1536]{1,0:T(8,128)(2,1)S(1)} %get-tuple-element.14), channel_id=1, source_target_pairs={{0,0},{5,1},{10,2},{19,3},{4,4},{9,5},{14,6},{23,7},{8,8},{13,9},{... | collective-permute-start | bytes 1179656 | tf_op jit(solution)/shard_map/ppermute | solution.py:41
  56.0 74.8 %collective-permute-start.4 = (bf16[128,1536]{1,0:T(8,128)(2,1)S(1)}, bf16[128,1536]{1,0:T(8,128)(2,1)S(1)}, u32[]{:S(2)}, u32[]{:S(2)}) collective-permute-start(bf16[128,1536]{1,0:T(8,128)(2,1)S(1)} %get-tuple-element.11), channel_id=1, source_target_pairs={{4,0},{9,1},{14,2},{19,3},{8,4},{13,5},{18,6},{23,7},{12,8},{17,9}... | collective-permute-start | bytes 1179656 | tf_op jit(solution)/shard_map/ppermute | solution.py:41
  58.2 72.6 %collective-permute-start.3 = (bf16[128,1536]{1,0:T(8,128)(2,1)S(1)}, bf16[128,1536]{1,0:T(8,128)(2,1)S(1)}, u32[]{:S(2)}, u32[]{:S(2)}) collective-permute-start(bf16[128,1536]{1,0:T(8,128)(2,1)S(1)} %get-tuple-element.12), channel_id=1, source_target_pairs={{0,0},{9,1},{14,2},{19,3},{4,4},{13,5},{18,6},{23,7},{8,8},{17,9},... | collective-permute-start | bytes 1179656 | tf_op jit(solution)/shard_map/ppermute | solution.py:41
  60.3 70.5 %copy-start.2 = (bf16[512,1536]{1,0:T(8,128)(2,1)S(1)}, bf16[512,1536]{1,0:T(8,128)(2,1)}, u32[]{:S(2)}) copy-start(bf16[512,1536]{1,0:T(8,128)(2,1)} %all-gather.2.cloned.1.call-done) | copy-start | bytes 4718596
  60.3 70.4 %collective-permute-start.2 = (bf16[128,1536]{1,0:T(8,128)(2,1)S(1)}, bf16[128,1536]{1,0:T(8,128)(2,1)S(1)}, u32[]{:S(2)}, u32[]{:S(2)}) collective-permute-start(bf16[128,1536]{1,0:T(8,128)(2,1)S(1)} %get-tuple-element.13), channel_id=1, source_target_pairs={{0,0},{5,1},{14,2},{19,3},{4,4},{9,5},{18,6},{23,7},{8,8},{13,9},{... | collective-permute-start | bytes 1179656 | tf_op jit(solution)/shard_map/ppermute | solution.py:41
Sparse Core Ops, SparseCore 0:
  27.2 19.8 all-gather.1
where the time goes:
time: 140 us
  waiting for transfers between devices  86.1 us (62%)
  blocking collectives  17.9 us (13%)
  starting transfers between devices  15.8 us (11%)
  between operations  13.6 us (10%)
  other arithmetic  2.56 us (2%)
  matrix products  2.47 us (2%)
  local copies, waits for them, and re-layouts  1.74 us (1%)
    ppermute x5, waiting for transfers between devices, rows_for_columns(): pieces.append(lax.ppermute(sent, ('samples', 'snps'), pairs))  66.1 us
    all_gather x1, waiting for transfers between devices, per_device(): full_rows = lax.all_gather(standard, 'snps', axis=1, tiled=True)  20 us
    psum x1, blocking collectives, per_device(): lax.psum((jnp.sum(dosage * observed_mask, axis=0), jnp.sum(observed_mask,...  17.9 us
    ppermute x5, starting transfers between devices, rows_for_columns(): pieces.append(lax.ppermute(sent, ('samples', 'snps'), pairs))  15.8 us
  transfers between devices with their start and end apart: 6, of which 3 were waited for; matrix products, arithmetic and copies ran while one was open for 0% of the time, Pallas kernels for 0%

commit v1 on v0

--- a/solution.py
+++ b/solution.py
@@ -50,7 +50,12 @@
     )
     standard = standardize(dosage, observed_mask, allele_sum, observed_sum)
     offsets = lax.axis_size("samples") // 2 + 1
-    full_rows = lax.all_gather(standard, "snps", axis=1, tiled=True)
+    ring = [standard]
+    for hop in range(3):
+        ring.append(lax.ppermute(ring[-1], "snps", [(dev, (dev + 1) % 4) for dev in range(4)]))
+    full_rows = jnp.roll(
+        jnp.concatenate(ring[::-1], axis=1), (lax.axis_index("snps") + 1) * ring[0].shape[1], axis=1
+    )
     others = rows_for_columns(full_rows, offsets)
     return cross_block(full_rows, others) / full_rows.shape[1]
 

time: 140 us -> 127 us (0.907)
  between operations: 13.6 us -> 0.15 us
  waiting for transfers between devices: 86.1 us -> 78.1 us
  starting transfers between devices: 15.8 us -> 22 us
    all_gather x1 -> x0, waiting for transfers between devices: 20 us -> none  [per_device(): full_rows = lax.all_gather(standard, 'snps', axis=1, tiled=True)]
    ppermute x0 -> x3, waiting for transfers between devices: none -> 14.2 us  [per_device(): lax.ppermute(ring[-1], 'snps', [(dev, (dev + 1) % 4) for dev in range(4)])]
    ppermute x0 -> x3, starting transfers between devices: none -> 9.58 us  [per_device(): lax.ppermute(ring[-1], 'snps', [(dev, (dev + 1) % 4) for dev in range(4)])]
    ppermute x5, starting transfers between devices: 15.8 us -> 12.4 us  [rows_for_columns(): pieces.append(lax.ppermute(sent, ('samples', 'snps'), pairs))]
    ppermute x5, waiting for transfers between devices: 66.1 us -> 64 us  [rows_for_columns(): pieces.append(lax.ppermute(sent, ('samples', 'snps'), pairs))]
  transfers between devices with their start and end apart: 6 -> 8, of which waited for: 3 -> 6; matrix products, arithmetic and copies ran while one was open for 0% -> 0% of each run, Pallas kernels for 0% -> 0%
where the time goes in v1:
time: 127 us; the launch traced here: 126 us
  waiting for transfers between devices  78.1 us (61%)
  starting transfers between devices  22 us (17%)
  blocking collectives  17.9 us (14%)
  other arithmetic  3.08 us (2%)
  matrix products  2.54 us (2%)
  local copies, waits for them, and re-layouts  2.03 us (2%)
    ppermute x5, waiting for transfers between devices, rows_for_columns(): pieces.append(lax.ppermute(sent, ('samples', 'snps'), pairs))  64 us
    psum x1, blocking collectives, per_device(): lax.psum((jnp.sum(dosage * observed_mask, axis=0), jnp.sum(observed_mask,...  17.9 us
    ppermute x3, waiting for transfers between devices, per_device(): lax.ppermute(ring[-1], 'snps', [(dev, (dev + 1) % 4) for dev in range(4)])  14.2 us
    ppermute x5, starting transfers between devices, rows_for_columns(): pieces.append(lax.ppermute(sent, ('samples', 'snps'), pairs))  12.4 us
    ppermute x3, starting transfers between devices, per_device(): lax.ppermute(ring[-1], 'snps', [(dev, (dev + 1) % 4) for dev in range(4)])  9.58 us
    dot_general x1, matrix products, cross_block(): lax.dot_general(own_rows, other_rows, (((1,), (1,)), ((), ())), preferred...  2.54 us
  transfers between devices with their start and end apart: 8, of which 6 were waited for; matrix products, arithmetic and copies ran while one was open for 0% of the time, Pallas kernels for 0%

profile of v1, /device:TPU:3, one launch (start us, length us, event | category | flops | bytes accessed | tf_op | source)
XLA Modules:
  0.0 125.8 jit_solution(12144615645415700399)
XLA Ops:
  0.0 1.5 %multiply_reduce_fusion = (f32[384]{0:T(512)S(1)}, f32[384]{0:T(512)S(1)}) fusion(s32[512,384]{1,0:T(8,128)} %param.2, s32[512,384]{1,0:T(8,128)} %param.3), kind=kLoop, calls=%fused_computation.4 | loop fusion | flops 982272 | bytes 1575936 | tf_op jit(solution)/shard_map/reduce_sum | solution.py:49
  1.5 17.9 %all-reduce = (f32[384]{0:T(512)S(1)}, f32[384]{0:T(512)S(1)}) all-reduce(f32[384]{0:T(512)S(1)} %get-tuple-element.6, f32[384]{0:T(512)S(1)} %get-tuple-element.5), channel_id=1, replica_groups=mesh['samples'=8,'snps'=4] {'samples'}, use_global_device_ids=true, to_apply=%region_3.0 | all-reduce | flops 768 | bytes 6144 | tf_op jit(solution)/shard_map/psum | solution.py:48
  19.5 1.5 %divide_convert_fusion = bf16[512,384]{1,0:T(8,128)(2,1)S(1)} fusion(s32[512,384]{1,0:T(8,128)} %param.2, s32[512,384]{1,0:T(8,128)} %param.3, f32[384]{0:T(512)S(1)} %multiply_sqrt_fusion, f32[384]{0:T(512)S(1)} %get-tuple-element.9), kind=kLoop, calls=%fused_computation.3 | loop fusion | flops 1179648 | bytes 1969152 | tf_op jit(solution)/shard_map/convert_element_type | solution.py:13
  21.0 4.6 %collective-permute-start = (bf16[512,384]{1,0:T(8,128)(2,1)S(1)}, bf16[512,384]{1,0:T(8,128)(2,1)S(1)}, u32[]{:S(2)}, u32[]{:S(2)}) collective-permute-start(bf16[512,384]{1,0:T(8,128)(2,1)S(1)} %divide_convert_fusion), channel_id=1, source_target_pairs={{0,1},{1,2},{2,3},{3,0},{4,5},{5,6},{6,7},{7,4},{8,9},{9,10},{10,1... | collective-permute-start | bytes 1179656 | tf_op jit(solution)/shard_map/ppermute | solution.py:55
  25.6 4.7 %collective-permute-done = bf16[512,384]{1,0:T(8,128)(2,1)S(1)} collective-permute-done((bf16[512,384]{1,0:T(8,128)(2,1)S(1)}, bf16[512,384]{1,0:T(8,128)(2,1)S(1)}, u32[]{:S(2)}, u32[]{:S(2)}) %collective-permute-start) | collective-permute-done | bytes 393248 | tf_op jit(solution)/shard_map/ppermute | solution.py:55
  30.3 2.5 %collective-permute-start.1 = (bf16[512,384]{1,0:T(8,128)(2,1)S(1)}, bf16[512,384]{1,0:T(8,128)(2,1)S(1)}, u32[]{:S(2)}, u32[]{:S(2)}) collective-permute-start(bf16[512,384]{1,0:T(8,128)(2,1)S(1)} %collective-permute-done), channel_id=1, source_target_pairs={{0,1},{1,2},{2,3},{3,0},{4,5},{5,6},{6,7},{7,4},{8,9},{9,10},{10,1... | collective-permute-start | bytes 1179656 | tf_op jit(solution)/shard_map/ppermute | solution.py:55
  32.8 4.7 %collective-permute-done.1 = bf16[512,384]{1,0:T(8,128)(2,1)S(1)} collective-permute-done((bf16[512,384]{1,0:T(8,128)(2,1)S(1)}, bf16[512,384]{1,0:T(8,128)(2,1)S(1)}, u32[]{:S(2)}, u32[]{:S(2)}) %collective-permute-start.1) | collective-permute-done | bytes 393248 | tf_op jit(solution)/shard_map/ppermute | solution.py:55
  37.6 2.5 %collective-permute-start.2 = (bf16[512,384]{1,0:T(8,128)(2,1)S(1)}, bf16[512,384]{1,0:T(8,128)(2,1)S(1)}, u32[]{:S(2)}, u32[]{:S(2)}) collective-permute-start(bf16[512,384]{1,0:T(8,128)(2,1)S(1)} %collective-permute-done.1), channel_id=1, source_target_pairs={{0,1},{1,2},{2,3},{3,0},{4,5},{5,6},{6,7},{7,4},{8,9},{9,10},{10,1... | collective-permute-start | bytes 1179656 | tf_op jit(solution)/shard_map/ppermute | solution.py:55
  40.0 4.7 %collective-permute-done.2 = bf16[512,384]{1,0:T(8,128)(2,1)S(1)} collective-permute-done((bf16[512,384]{1,0:T(8,128)(2,1)S(1)}, bf16[512,384]{1,0:T(8,128)(2,1)S(1)}, u32[]{:S(2)}, u32[]{:S(2)}) %collective-permute-start.2) | collective-permute-done | bytes 393248 | tf_op jit(solution)/shard_map/ppermute | solution.py:55
  44.8 0.1 constant_dynamic-update-slice_fusion.7
  44.8 0.1 constant_dynamic-update-slice_fusion.6
  44.9 0.1 constant_dynamic-update-slice_fusion.5
  45.0 0.1 constant_dynamic-update-slice_fusion.4
  45.1 0.1 constant_dynamic-update-slice_fusion.3
  45.2 0.1 constant_dynamic-update-slice_fusion.2
  45.3 0.1 constant_dynamic-update-slice_fusion.1
  45.4 0.1 constant_dynamic-update-slice_fusion
  45.5 1.2 fusion.6
  46.7 1.9 %collective-permute-start.3 = (bf16[128,1536]{1,0:T(8,128)(2,1)S(1)}, bf16[128,1536]{1,0:T(8,128)(2,1)S(1)}, u32[]{:S(2)}, u32[]{:S(2)}) collective-permute-start(bf16[128,1536]{1,0:T(8,128)(2,1)S(1)} %get-tuple-element.15), channel_id=1, source_target_pairs={{0,0},{5,1},{10,2},{15,3},{4,4},{9,5},{14,6},{19,7},{8,8},{13,9},{... | collective-permute-start | bytes 1179656 | tf_op jit(solution)/shard_map/ppermute | solution.py:41
  48.6 1.9 %collective-permute-start.4 = (bf16[128,1536]{1,0:T(8,128)(2,1)S(1)}, bf16[128,1536]{1,0:T(8,128)(2,1)S(1)}, u32[]{:S(2)}, u32[]{:S(2)}) collective-permute-start(bf16[128,1536]{1,0:T(8,128)(2,1)S(1)} %get-tuple-element.14), channel_id=1, source_target_pairs={{0,0},{5,1},{10,2},{19,3},{4,4},{9,5},{14,6},{23,7},{8,8},{13,9},{... | collective-permute-start | bytes 1179656 | tf_op jit(solution)/shard_map/ppermute | solution.py:41
  50.6 2.4 %collective-permute-start.7 = (bf16[128,1536]{1,0:T(8,128)(2,1)S(1)}, bf16[128,1536]{1,0:T(8,128)(2,1)S(1)}, u32[]{:S(2)}, u32[]{:S(2)}) collective-permute-start(bf16[128,1536]{1,0:T(8,128)(2,1)S(1)} %get-tuple-element.11), channel_id=1, source_target_pairs={{4,0},{9,1},{14,2},{19,3},{8,4},{13,5},{18,6},{23,7},{12,8},{17,9}... | collective-permute-start | bytes 1179656 | tf_op jit(solution)/shard_map/ppermute | solution.py:41
  53.0 1.9 %collective-permute-start.6 = (bf16[128,1536]{1,0:T(8,128)(2,1)S(1)}, bf16[128,1536]{1,0:T(8,128)(2,1)S(1)}, u32[]{:S(2)}, u32[]{:S(2)}) collective-permute-start(bf16[128,1536]{1,0:T(8,128)(2,1)S(1)} %get-tuple-element.12), channel_id=1, source_target_pairs={{0,0},{9,1},{14,2},{19,3},{4,4},{13,5},{18,6},{23,7},{8,8},{17,9},... | collective-permute-start | bytes 1179656 | tf_op jit(solution)/shard_map/ppermute | solution.py:41
  54.9 4.2 %collective-permute-start.5 = (bf16[128,1536]{1,0:T(8,128)(2,1)S(1)}, bf16[128,1536]{1,0:T(8,128)(2,1)S(1)}, u32[]{:S(2)}, u32[]{:S(2)}) collective-permute-start(bf16[128,1536]{1,0:T(8,128)(2,1)S(1)} %get-tuple-element.13), channel_id=1, source_target_pairs={{0,0},{5,1},{14,2},{19,3},{4,4},{9,5},{18,6},{23,7},{8,8},{13,9},{... | collective-permute-start | bytes 1179656 | tf_op jit(solution)/shard_map/ppermute | solution.py:41
  59.2 1.2 collective-permute-done.3
  60.4 37.5 %collective-permute-done.4 = bf16[128,1536]{1,0:T(8,128)(2,1)S(1)} collective-permute-done((bf16[128,1536]{1,0:T(8,128)(2,1)S(1)}, bf16[128,1536]{1,0:T(8,128)(2,1)S(1)}, u32[]{:S(2)}, u32[]{:S(2)}) %collective-permute-start.4) | collective-permute-done | bytes 393248 | tf_op jit(solution)/shard_map/ppermute | solution.py:41
  97.9 25.2 %collective-permute-done.5 = bf16[128,1536]{1,0:T(8,128)(2,1)S(1)} collective-permute-done((bf16[128,1536]{1,0:T(8,128)(2,1)S(1)}, bf16[128,1536]{1,0:T(8,128)(2,1)S(1)}, u32[]{:S(2)}, u32[]{:S(2)}) %collective-permute-start.5) | collective-permute-done | bytes 393248 | tf_op jit(solution)/shard_map/ppermute | solution.py:41
  123.2 0.0 collective-permute-done.6
  123.3 0.0 collective-permute-done.7
  123.3 2.5 %fusion.2 = f32[512,640]{1,0:T(8,128)} fusion(bf16[640,1536]{1,0:T(8,128)(2,1)S(1)} %constant_dynamic-update-slice_fusion.8, bf16[512,3072]{1,0:T(8,128)(2,1)S(1)} %constant_dynamic-update-slice_fusion, s32[]{:T(128)S(6)} %select_n.63), kind=kOutput, calls=%fused_computation.2 | convolution fusion | flops 1006960640 | bytes 4849668 | tf_op jit(solution)/shard_map/dot_general | solution.py:17
  (7 shorter events, 0.2 us)
Async XLA Ops:
  21.0 9.3 %collective-permute-start = (bf16[512,384]{1,0:T(8,128)(2,1)S(1)}, bf16[512,384]{1,0:T(8,128)(2,1)S(1)}, u32[]{:S(2)}, u32[]{:S(2)}) collective-permute-start(bf16[512,384]{1,0:T(8,128)(2,1)S(1)} %divide_convert_fusion), channel_id=1, source_target_pairs={{0,1},{1,2},{2,3},{3,0},{4,5},{5,6},{6,7},{7,4},{8,9},{9,10},{10,1... | collective-permute-start | bytes 1179656 | tf_op jit(solution)/shard_map/ppermute | solution.py:55
  30.3 7.2 %collective-permute-start.1 = (bf16[512,384]{1,0:T(8,128)(2,1)S(1)}, bf16[512,384]{1,0:T(8,128)(2,1)S(1)}, u32[]{:S(2)}, u32[]{:S(2)}) collective-permute-start(bf16[512,384]{1,0:T(8,128)(2,1)S(1)} %collective-permute-done), channel_id=1, source_target_pairs={{0,1},{1,2},{2,3},{3,0},{4,5},{5,6},{6,7},{7,4},{8,9},{9,10},{10,1... | collective-permute-start | bytes 1179656 | tf_op jit(solution)/shard_map/ppermute | solution.py:55
  37.6 7.2 %collective-permute-start.2 = (bf16[512,384]{1,0:T(8,128)(2,1)S(1)}, bf16[512,384]{1,0:T(8,128)(2,1)S(1)}, u32[]{:S(2)}, u32[]{:S(2)}) collective-permute-start(bf16[512,384]{1,0:T(8,128)(2,1)S(1)} %collective-permute-done.1), channel_id=1, source_target_pairs={{0,1},{1,2},{2,3},{3,0},{4,5},{5,6},{6,7},{7,4},{8,9},{9,10},{10,1... | collective-permute-start | bytes 1179656 | tf_op jit(solution)/shard_map/ppermute | solution.py:55
  46.7 13.6 %collective-permute-start.3 = (bf16[128,1536]{1,0:T(8,128)(2,1)S(1)}, bf16[128,1536]{1,0:T(8,128)(2,1)S(1)}, u32[]{:S(2)}, u32[]{:S(2)}) collective-permute-start(bf16[128,1536]{1,0:T(8,128)(2,1)S(1)} %get-tuple-element.15), channel_id=1, source_target_pairs={{0,0},{5,1},{10,2},{15,3},{4,4},{9,5},{14,6},{19,7},{8,8},{13,9},{... | collective-permute-start | bytes 1179656 | tf_op jit(solution)/shard_map/ppermute | solution.py:41
  48.6 49.2 %collective-permute-start.4 = (bf16[128,1536]{1,0:T(8,128)(2,1)S(1)}, bf16[128,1536]{1,0:T(8,128)(2,1)S(1)}, u32[]{:S(2)}, u32[]{:S(2)}) collective-permute-start(bf16[128,1536]{1,0:T(8,128)(2,1)S(1)} %get-tuple-element.14), channel_id=1, source_target_pairs={{0,0},{5,1},{10,2},{19,3},{4,4},{9,5},{14,6},{23,7},{8,8},{13,9},{... | collective-permute-start | bytes 1179656 | tf_op jit(solution)/shard_map/ppermute | solution.py:41
  50.6 72.7 %collective-permute-start.7 = (bf16[128,1536]{1,0:T(8,128)(2,1)S(1)}, bf16[128,1536]{1,0:T(8,128)(2,1)S(1)}, u32[]{:S(2)}, u32[]{:S(2)}) collective-permute-start(bf16[128,1536]{1,0:T(8,128)(2,1)S(1)} %get-tuple-element.11), channel_id=1, source_target_pairs={{4,0},{9,1},{14,2},{19,3},{8,4},{13,5},{18,6},{23,7},{12,8},{17,9}... | collective-permute-start | bytes 1179656 | tf_op jit(solution)/shard_map/ppermute | solution.py:41
  53.0 70.2 %collective-permute-start.6 = (bf16[128,1536]{1,0:T(8,128)(2,1)S(1)}, bf16[128,1536]{1,0:T(8,128)(2,1)S(1)}, u32[]{:S(2)}, u32[]{:S(2)}) collective-permute-start(bf16[128,1536]{1,0:T(8,128)(2,1)S(1)} %get-tuple-element.12), channel_id=1, source_target_pairs={{0,0},{9,1},{14,2},{19,3},{4,4},{13,5},{18,6},{23,7},{8,8},{17,9},... | collective-permute-start | bytes 1179656 | tf_op jit(solution)/shard_map/ppermute | solution.py:41
  54.9 68.3 %collective-permute-start.5 = (bf16[128,1536]{1,0:T(8,128)(2,1)S(1)}, bf16[128,1536]{1,0:T(8,128)(2,1)S(1)}, u32[]{:S(2)}, u32[]{:S(2)}) collective-permute-start(bf16[128,1536]{1,0:T(8,128)(2,1)S(1)} %get-tuple-element.13), channel_id=1, source_target_pairs={{0,0},{5,1},{14,2},{19,3},{4,4},{9,5},{18,6},{23,7},{8,8},{13,9},{... | collective-permute-start | bytes 1179656 | tf_op jit(solution)/shard_map/ppermute | solution.py:41
